TPU v7x, 32 devices: a whole 2x2x4 slice. The times are simulated.
32 devices in a mesh: mem: 4 (over z), tile: 8 (over y, x, core).
Axes of the slice: x: 2, y: 2, z: 4, core: 2. Of those that a mesh axis runs over, the one named last changes fastest.
Arguments:
- alpha: float32 [32, 8, 192, 384], P('mem', None, 'tile'), may hold values from -6 to 6
- ensemble: bfloat16 [2, 32, 8, 192, 384], P(None, 'mem', None, 'tile'), may hold values from -1 to 1
- innovation: float32 [2, 8, 192, 384], P(None, None, 'tile'), may hold values from -6 to 6
- precision: float32 [2, 8, 192, 384], P(None, None, 'tile'), may hold values from 0.5 to 8
- diffusivity: float32 [2, 8, 192, 384], P(None, None, 'tile'), may hold values from 0.01 to 0.48, as said below
Outputs:
- gradient: float32 [32, 8, 192, 384], P('mem', None, 'tile')
- increment: float32 [2, 8, 192, 384], P(None, None, 'tile')
Inputs may be any that keep to these rules, and one draw needn't show every extreme that they name: diffusivity[0] lies between 0.40 and 0.48 and diffusivity[1] between 0.01 and 0.02, so the four faces of a cell sum to at most 1.
All inputs are finite; a program needn't handle non-finite values.
Results may differ from a plain program's by a relative error of at most 0.0003.
Values sent between devices are 32-bit elements; how exact they have to be, the bound alone decides.
A program may use at most 64 MiB of HBM per device.

v0:
```python
import jax
import jax.numpy as jnp
from jax import lax
from jax.sharding import PartitionSpec as P

STEPS = 4


def extended(cells, sides, width):
    for axis, dim in sides:
        count = lax.axis_size(axis)
        head = lax.slice_in_dim(cells, 0, width, axis=dim)
        tail = lax.slice_in_dim(cells, cells.shape[dim] - width, cells.shape[dim], axis=dim)
        cells = jnp.concatenate(
            [
                lax.ppermute(tail, axis, [(i, (i + 1) % count) for i in range(count)]),
                cells,
                lax.ppermute(head, axis, [((i + 1) % count, i) for i in range(count)]),
            ],
            axis=dim,
        )
    return cells


def diffuse(field, coeffs, width):
    for sweep in range(width):
        columns = field.shape[2]
        zonal_face = coeffs[0, :, sweep : sweep + columns - 1]
        merid_face = coeffs[1, :, sweep + 1 : sweep + columns - 1]
        zonal_flux = zonal_face * (field[:, :, 1:] - field[:, :, :-1])
        interior = field[:, :, 1:-1]
        merid_flux = merid_face[:, :, :-1] * (interior[:, :, :, 1:] - interior[:, :, :, :-1])
        padding = jnp.zeros_like(interior[:, :, :, :1])
        north_flux = jnp.concatenate([merid_flux, padding], axis=3)
        south_flux = jnp.concatenate([padding, merid_flux], axis=3)
        field = interior + zonal_flux[:, :, 1:] - zonal_flux[:, :, :-1] + north_flux - south_flux
    return field


def per_device(alpha, ensemble, innovation, precision, diffusivity):
    coeffs = extended(diffusivity, (("tile", 2),), STEPS)
    padded = extended(alpha, (("tile", 2),), STEPS)
    localized = diffuse(padded, coeffs, STEPS)
    partial_sum = jnp.sum(ensemble.astype(jnp.float32) * localized[None], axis=1)
    increment = lax.psum(partial_sum, "mem")
    weighted = precision * (increment - innovation)
    projected = jnp.sum(ensemble.astype(jnp.float32) * weighted[:, None], axis=0)
    padded_adj = extended(projected, (("tile", 2),), STEPS)
    adjoint_field = diffuse(padded_adj, coeffs, STEPS)
    gradient = alpha + adjoint_field
    return (gradient, increment)


def solution(mesh):
    in_specs = (
        P("mem", None, "tile", None),
        P(None, "mem", None, "tile", None),
        P(None, None, "tile", None),
        P(None, None, "tile", None),
        P(None, None, "tile", None),
    )
    out_specs = (P("mem", None, "tile", None), P(None, None, "tile", None))
    return jax.shard_map(
        per_device, mesh=mesh, in_specs=in_specs, out_specs=out_specs, check_vma=False
    )
```

profile of v0, /device:TPU:1, one launch (start us, length us, event | category | flops | bytes accessed | tf_op | source)
XLA Modules:
  0.0 121.3 jit_solution(3033836365526358352)
XLA Ops:
  7.2 1.1 fusion.38
  8.3 2.6 %collective-permute-start.2 = (f32[2,8,4,384]{3,2,1,0:T(4,128)S(1)}, f32[2,8,4,384]{3,2,1,0:T(4,128)S(1)}, u32[]{:S(2)}, u32[]{:S(2)}) collective-permute-start(f32[2,8,4,384]{3,2,1,0:T(4,128)S(1)} %get-tuple-element.8), channel_id=1, source_target_pairs={{0,1},{1,2},{2,3},{3,4},{4,5},{5,6},{6,7},{7,0},{8,9},{9,10},{10,1... | collective-permute-start | bytes 294920 | tf_op jit(solution)/shard_map/ppermute | solution.py:16
  11.0 1.5 %fusion.37 = (f32[8,8,4,384]{3,2,1,0:T(4,128)S(1)}, f32[8,8,4,384]{3,2,1,0:T(4,128)S(1)}) fusion(f32[8,8,24,384]{3,2,1,0:T(8,128)} %param.5), kind=kLoop, calls=%fused_computation.83 | loop fusion | bytes 1572864 | tf_op jit(solution)/shard_map/slice | solution.py:13
  12.5 1.8 %collective-permute-start = (f32[8,8,4,384]{3,1,2,0:T(8,128)S(1)}, f32[8,8,4,384]{3,1,2,0:T(8,128)S(1)}, u32[]{:S(2)}, u32[]{:S(2)}) collective-permute-start(f32[8,8,4,384]{3,1,2,0:T(8,128)S(1)} %copy.29), channel_id=1, source_target_pairs={{0,1},{1,2},{2,3},{3,4},{4,5},{5,6},{6,7},{7,0},{8,9},{9,10},{10,1... | collective-permute-start | bytes 1179656 | tf_op jit(solution)/shard_map/ppermute | solution.py:16
  15.5 0.8 slice_bitcast_fusion.2
  17.0 0.8 slice_bitcast_fusion
  17.9 0.8 slice_bitcast_fusion.1
  18.6 2.6 %collective-permute-done = f32[8,8,4,384]{3,1,2,0:T(8,128)S(1)} collective-permute-done((f32[8,8,4,384]{3,1,2,0:T(8,128)S(1)}, f32[8,8,4,384]{3,1,2,0:T(8,128)S(1)}, u32[]{:S(2)}, u32[]{:S(2)}) %collective-permute-start) | collective-permute-done | bytes 393248 | tf_op jit(solution)/shard_map/ppermute | solution.py:16
  21.4 4.5 %collective-permute-done.1 = f32[8,8,4,384]{3,1,2,0:T(8,128)S(1)} collective-permute-done((f32[8,8,4,384]{3,1,2,0:T(8,128)S(1)}, f32[8,8,4,384]{3,1,2,0:T(8,128)S(1)}, u32[]{:S(2)}, u32[]{:S(2)}) %collective-permute-start.1) | collective-permute-done | bytes 393248 | tf_op jit(solution)/shard_map/ppermute | solution.py:18
  26.5 1.2 fusion.24
  28.2 1.7 %fusion.26 = f32[8,8,30,384]{3,2,1,0:T(8,128)S(1)} fusion(f32[8,8,31,384]{3,2,1,0:T(8,128)S(1)} %fusion.27, f32[8,8,32,384]{3,2,1,0:T(8,128)S(1)} %pad_maximum_fusion, f32[8,8,30,383]{3,2,1,0:T(8,128)S(1)} %fusion.24), kind=kLoop, calls=%fused_computation.52 | loop fusion | flops 2949120 | bytes 14737920 | tf_op jit(solution)/shard_map/sub | solution.py:36
  29.9 1.2 fusion.20
  31.7 1.7 %fusion.22 = f32[8,8,28,384]{3,2,1,0:T(8,128)S(1)} fusion(f32[8,8,29,384]{3,2,1,0:T(8,128)S(1)} %fusion.23, f32[8,8,30,384]{3,2,1,0:T(8,128)S(1)} %fusion.26, f32[8,8,28,383]{3,2,1,0:T(8,128)S(1)} %fusion.20), kind=kLoop, calls=%fused_computation.44 | loop fusion | flops 2752512 | bytes 13755392 | tf_op jit(solution)/shard_map/sub | solution.py:36
  33.4 1.2 fusion.16
  35.2 1.7 %fusion.18 = f32[8,8,26,384]{3,2,1,0:T(8,128)S(1)} fusion(f32[8,8,27,384]{3,2,1,0:T(8,128)S(1)} %fusion.19, f32[8,8,28,384]{3,2,1,0:T(8,128)S(1)} %fusion.22, f32[8,8,26,383]{3,2,1,0:T(8,128)S(1)} %fusion.16), kind=kLoop, calls=%fused_computation.36 | loop fusion | flops 2555904 | bytes 12772864 | tf_op jit(solution)/shard_map/sub | solution.py:36
  37.8 1.1 fusion.32
  38.9 1.2 fusion.34
  40.6 1.3 %fusion = f32[2,8,24,384]{3,2,1,0:T(8,128)} fusion(bf16[2,8,8,24,384]{4,3,2,1,0:T(8,128)(2,1)S(1)} %copy-done.1, f32[8,8,24,384]{3,2,1,0:T(8,128)S(1)} %fusion.34), kind=kLoop, calls=%fused_computation.2 | loop fusion | flops 3391488 | bytes 5308416 | tf_op jit(solution)/shard_map/reduce_sum | solution.py:44
  41.9 39.6 %all-reduce.18.cloned.1.call-done = f32[2,8,24,384]{3,2,1,0:T(8,128)} async-done(((f32[2,8,24,384]{3,2,1,0:T(8,128)}), f32[2,8,24,384]{3,2,1,0:T(8,128)}) %all-reduce.18.cloned.1.call-update) | async-done | bytes 589840 | tf_op jit(solution)/shard_map/psum | solution.py:45
  81.5 1.6 %subtract_multiply_fusion = f32[2,8,24,384]{3,2,1,0:T(8,128)S(1)} fusion(f32[2,8,24,384]{3,2,1,0:T(8,128)} %param.8, f32[2,8,24,384]{3,2,1,0:T(8,128)} %all-reduce.18.cloned.1.call-done, f32[2,8,24,384]{3,2,1,0:T(8,128)} %param.7), kind=kLoop, calls=%fused_computation.72 | loop fusion | flops 294912 | bytes 2359296 | tf_op jit(solution)/shard_map/mul | solution.py:46
  84.4 2.4 %collective-permute-start.4 = (f32[8,8,4,384]{3,1,2,0:T(8,128)S(1)}, f32[8,8,4,384]{3,1,2,0:T(8,128)S(1)}, u32[]{:S(2)}, u32[]{:S(2)}) collective-permute-start(f32[8,8,4,384]{3,1,2,0:T(8,128)S(1)} %copy.25), channel_id=1, source_target_pairs={{0,1},{1,2},{2,3},{3,4},{4,5},{5,6},{6,7},{7,0},{8,9},{9,10},{10,1... | collective-permute-start | bytes 1179656 | tf_op jit(solution)/shard_map/ppermute | solution.py:16
  87.0 7.0 %collective-permute-done.4 = f32[8,8,4,384]{3,1,2,0:T(8,128)S(1)} collective-permute-done((f32[8,8,4,384]{3,1,2,0:T(8,128)S(1)}, f32[8,8,4,384]{3,1,2,0:T(8,128)S(1)}, u32[]{:S(2)}, u32[]{:S(2)}) %collective-permute-start.4) | collective-permute-done | bytes 393248 | tf_op jit(solution)/shard_map/ppermute | solution.py:16
  94.1 3.4 %collective-permute-done.5 = f32[8,8,4,384]{3,1,2,0:T(8,128)S(1)} collective-permute-done((f32[8,8,4,384]{3,1,2,0:T(8,128)S(1)}, f32[8,8,4,384]{3,1,2,0:T(8,128)S(1)}, u32[]{:S(2)}, u32[]{:S(2)}) %collective-permute-start.5) | collective-permute-done | bytes 393248 | tf_op jit(solution)/shard_map/ppermute | solution.py:18
  98.5 1.2 fusion.11
  100.2 1.7 %fusion.13 = f32[8,8,30,384]{3,2,1,0:T(8,128)S(1)} fusion(f32[8,8,31,384]{3,2,1,0:T(8,128)S(1)} %fusion.14, f32[8,8,32,384]{3,2,1,0:T(8,128)S(1)} %pad_maximum_fusion.1, f32[8,8,30,383]{3,2,1,0:T(8,128)S(1)} %fusion.11), kind=kLoop, calls=%fused_computation.26 | loop fusion | flops 2949120 | bytes 14737920 | tf_op jit(solution)/shard_map/sub | solution.py:36
  102.0 1.2 fusion.7
  103.7 1.7 %fusion.9 = f32[8,8,28,384]{3,2,1,0:T(8,128)S(1)} fusion(f32[8,8,29,384]{3,2,1,0:T(8,128)S(1)} %fusion.10, f32[8,8,30,384]{3,2,1,0:T(8,128)S(1)} %fusion.13, f32[8,8,28,383]{3,2,1,0:T(8,128)S(1)} %fusion.7), kind=kLoop, calls=%fused_computation.18 | loop fusion | flops 2752512 | bytes 13755392 | tf_op jit(solution)/shard_map/sub | solution.py:36
  105.4 1.2 fusion.3
  107.2 1.7 %fusion.5 = f32[8,8,26,384]{3,2,1,0:T(8,128)S(1)} fusion(f32[8,8,27,384]{3,2,1,0:T(8,128)S(1)} %fusion.6, f32[8,8,28,384]{3,2,1,0:T(8,128)S(1)} %fusion.9, f32[8,8,26,383]{3,2,1,0:T(8,128)S(1)} %fusion.3), kind=kLoop, calls=%fused_computation.10 | loop fusion | flops 2555904 | bytes 12772864 | tf_op jit(solution)/shard_map/sub | solution.py:36
  109.8 0.9 fusion.28
  110.8 2.9 %fusion.31 = f32[8,8,24,384]{3,2,1,0:T(8,128)} fusion(f32[8,8,24,384]{3,2,1,0:T(8,128)S(1)} %copy-done, f32[8,8,25,384]{3,2,1,0:T(8,128)S(1)} %fusion.2, f32[8,8,26,384]{3,2,1,0:T(8,128)S(1)} %fusion.5, f32[8,8,24,383]{3,2,1,0:T(8,128)S(1)} %fusion.28), kind=kLoop, calls=%fused_computation.63 | loop fusion | flops 2949120 | bytes 14149632 | tf_op jit(solution)/shard_map/add | solution.py:50
  113.7 0.8 copy.32
  (67 shorter events, 10.8 us)
Async XLA Ops:
  7.2 7.3 %copy-start.3 = (f32[2,8,24,384]{3,2,1,0:T(8,128)S(1)}, f32[2,8,24,384]{3,2,1,0:T(8,128)}, u32[]{:S(2)}) copy-start(f32[2,8,24,384]{3,2,1,0:T(8,128)} %param.9) | copy-start | bytes 1769476
  7.2 74.3 %all-reduce.18.cloned.1.call-start = ((), (), s32[]{:S(2)}) async-start(), calls=%async_computation | async-start | bytes 1179648 | tf_op jit(solution)/shard_map/psum | solution.py:45
  8.3 6.9 %collective-permute-start.2 = (f32[2,8,4,384]{3,2,1,0:T(4,128)S(1)}, f32[2,8,4,384]{3,2,1,0:T(4,128)S(1)}, u32[]{:S(2)}, u32[]{:S(2)}) collective-permute-start(f32[2,8,4,384]{3,2,1,0:T(4,128)S(1)} %get-tuple-element.8), channel_id=1, source_target_pairs={{0,1},{1,2},{2,3},{3,4},{4,5},{5,6},{6,7},{7,0},{8,9},{9,10},{10,1... | collective-permute-start | bytes 294920 | tf_op jit(solution)/shard_map/ppermute | solution.py:16
  11.0 4.3 %collective-permute-start.3 = (f32[2,8,4,384]{3,2,1,0:T(4,128)S(1)}, f32[2,8,4,384]{3,2,1,0:T(4,128)S(1)}, u32[]{:S(2)}, u32[]{:S(2)}) collective-permute-start(f32[2,8,4,384]{3,2,1,0:T(4,128)S(1)} %get-tuple-element.9), channel_id=1, source_target_pairs={{1,0},{2,1},{3,2},{4,3},{5,4},{6,5},{7,6},{0,7},{9,8},{10,9},{11,1... | collective-permute-start | bytes 294920 | tf_op jit(solution)/shard_map/ppermute | solution.py:18
  12.5 8.7 %collective-permute-start = (f32[8,8,4,384]{3,1,2,0:T(8,128)S(1)}, f32[8,8,4,384]{3,1,2,0:T(8,128)S(1)}, u32[]{:S(2)}, u32[]{:S(2)}) collective-permute-start(f32[8,8,4,384]{3,1,2,0:T(8,128)S(1)} %copy.29), channel_id=1, source_target_pairs={{0,1},{1,2},{2,3},{3,4},{4,5},{5,6},{6,7},{7,0},{8,9},{9,10},{10,1... | collective-permute-start | bytes 1179656 | tf_op jit(solution)/shard_map/ppermute | solution.py:16
  14.4 11.5 %collective-permute-start.1 = (f32[8,8,4,384]{3,1,2,0:T(8,128)S(1)}, f32[8,8,4,384]{3,1,2,0:T(8,128)S(1)}, u32[]{:S(2)}, u32[]{:S(2)}) collective-permute-start(f32[8,8,4,384]{3,1,2,0:T(8,128)S(1)} %copy.30), channel_id=1, source_target_pairs={{1,0},{2,1},{3,2},{4,3},{5,4},{6,5},{7,6},{0,7},{9,8},{10,9},{11,1... | collective-permute-start | bytes 1179656 | tf_op jit(solution)/shard_map/ppermute | solution.py:18
  15.4 11.1 %copy-start.12 = (f32[8,30,384]{2,1,0:T(8,128)}, f32[8,30,384]{2,1,0:T(8,128)S(1)}, u32[]{:S(2)}) copy-start(f32[8,30,384]{2,1,0:T(8,128)S(1)} %slice_bitcast_fusion.4) | copy-start | bytes 1105924
  15.4 10.5 %copy-start = (f32[8,8,24,384]{3,2,1,0:T(8,128)S(1)}, f32[8,8,24,384]{3,2,1,0:T(8,128)}, u32[]{:S(2)}) copy-start(f32[8,8,24,384]{3,2,1,0:T(8,128)} %param.5) | copy-start | bytes 7077892
  15.5 12.2 %copy-start.10 = (f32[8,31,384]{2,1,0:T(8,128)}, f32[8,31,384]{2,1,0:T(8,128)S(1)}, u32[]{:S(2)}) copy-start(f32[8,31,384]{2,1,0:T(8,128)S(1)} %slice_bitcast_fusion.5) | copy-start | bytes 1142788
  28.2 1.7 %copy-start.9 = (f32[8,28,384]{2,1,0:T(8,128)S(1)}, f32[8,28,384]{2,1,0:T(8,128)}, u32[]{:S(2)}) copy-start(f32[8,28,384]{2,1,0:T(8,128)} %slice_bitcast_fusion.2) | copy-start | bytes 1032196
  29.9 1.2 copy-start.7
  31.7 1.7 %copy-start.4 = (f32[8,26,384]{2,1,0:T(8,128)S(1)}, f32[8,26,384]{2,1,0:T(8,128)}, u32[]{:S(2)}) copy-start(f32[8,26,384]{2,1,0:T(8,128)} %slice_bitcast_fusion) | copy-start | bytes 958468
  33.4 1.2 copy-start.5
  36.9 1.0 copy-start.14
  38.9 1.7 %copy-start.1 = (bf16[2,8,8,24,384]{4,3,2,1,0:T(8,128)(2,1)S(1)}, bf16[2,8,8,24,384]{4,3,2,1,0:T(8,128)(2,1)}, u32[]{:S(2)}) copy-start(bf16[2,8,8,24,384]{4,3,2,1,0:T(8,128)(2,1)} %param.6) | copy-start | bytes 7077892
  81.5 2.2 %copy-start.2 = (bf16[2,8,8,24,384]{4,3,2,1,0:T(8,128)(2,1)S(1)}, bf16[2,8,8,24,384]{4,3,2,1,0:T(8,128)(2,1)}, u32[]{:S(2)}) copy-start(bf16[2,8,8,24,384]{4,3,2,1,0:T(8,128)(2,1)} %param.6) | copy-start | bytes 7077892
  84.4 9.5 %collective-permute-start.4 = (f32[8,8,4,384]{3,1,2,0:T(8,128)S(1)}, f32[8,8,4,384]{3,1,2,0:T(8,128)S(1)}, u32[]{:S(2)}, u32[]{:S(2)}) collective-permute-start(f32[8,8,4,384]{3,1,2,0:T(8,128)S(1)} %copy.25), channel_id=1, source_target_pairs={{0,1},{1,2},{2,3},{3,4},{4,5},{5,6},{6,7},{7,0},{8,9},{9,10},{10,1... | collective-permute-start | bytes 1179656 | tf_op jit(solution)/shard_map/ppermute | solution.py:16
  86.9 10.5 %collective-permute-start.5 = (f32[8,8,4,384]{3,1,2,0:T(8,128)S(1)}, f32[8,8,4,384]{3,1,2,0:T(8,128)S(1)}, u32[]{:S(2)}, u32[]{:S(2)}) collective-permute-start(f32[8,8,4,384]{3,1,2,0:T(8,128)S(1)} %copy.26), channel_id=1, source_target_pairs={{1,0},{2,1},{3,2},{4,3},{5,4},{6,5},{7,6},{0,7},{9,8},{10,9},{11,1... | collective-permute-start | bytes 1179656 | tf_op jit(solution)/shard_map/ppermute | solution.py:18
  97.5 1.0 copy-start.13
  98.5 1.2 copy-start.11
  102.0 1.2 copy-start.8
  105.4 1.2 copy-start.6
  108.9 1.0 copy-start.15
  110.8 2.9 %copy-start.16 = (f32[2,8,24,384]{3,2,1,0:T(8,128)S(1)}, f32[2,8,24,384]{3,2,1,0:T(8,128)}, u32[]{:S(2)}) copy-start(f32[2,8,24,384]{3,2,1,0:T(8,128)} %all-reduce.18.cloned.1.call-done) | copy-start | bytes 1769476
Sparse Core Ops, SparseCore 0:
  42.1 39.3 all-reduce.17
where the time goes:
time: 122 us; the launch traced here: 121 us
  waiting for transfers between devices  57 us (47%)
  other arithmetic  32.3 us (26%)
  between operations  14.5 us (12%)
  local copies, waits for them, and re-layouts  10.5 us (9%)
  starting transfers between devices  7.02 us (6%)
    psum x1, waiting for transfers between devices, per_device(): increment = lax.psum(partial_sum, 'mem')  39.6 us
    sub x7, other arithmetic, diffuse(): interior + zonal_flux[:, :, 1:] - zonal_flux[:, :, :-1] + north_flux  11.5 us
    ppermute x3, waiting for transfers between devices, extended(): lax.ppermute(tail, axis, [(i, (i + 1) % count) for i in range(count)])  9.61 us
    mul x8, other arithmetic, diffuse(): merid_face[:, :, :-1] * (interior[:, :, :, 1:] - interior[:, :, :, :-1])  9.07 us
    ppermute x3, waiting for transfers between devices, extended(): lax.ppermute(head, axis, [((i + 1) % count, i) for i in range(count)])  7.86 us
    ppermute x3, starting transfers between devices, extended(): lax.ppermute(tail, axis, [(i, (i + 1) % count) for i in range(count)])  6.86 us
    mul x9, other arithmetic, diffuse(): zonal_flux = zonal_face * (field[:, :, 1:] - field[:, :, :-1])  4.23 us
    unnamed x37, local copies, waits for them, and re-layouts  3.27 us
  transfers between devices with their start and end apart: 7, of which 5 were waited for; matrix products, arithmetic and copies ran while one was open for 5% of the time, Pallas kernels for 0%

commit v1 on v0

--- a/solution.py
+++ b/solution.py
@@ -42,7 +42,7 @@
     padded = extended(alpha, (("tile", 2),), STEPS)
     localized = diffuse(padded, coeffs, STEPS)
     partial_sum = jnp.sum(ensemble.astype(jnp.float32) * localized[None], axis=1)
-    increment = lax.psum(partial_sum, "mem")
+    increment = jnp.sum(lax.all_gather(partial_sum, "mem"), axis=0)
     weighted = precision * (increment - innovation)
     projected = jnp.sum(ensemble.astype(jnp.float32) * weighted[:, None], axis=0)
     padded_adj = extended(projected, (("tile", 2),), STEPS)

time: 122 us -> 134 us (1.098)
  waiting for transfers between devices: 57 us -> 67.8 us
  other arithmetic: 32.3 us -> 34.9 us
    all_gather x0 -> x1, waiting for transfers between devices: none -> 50.4 us  [per_device(): increment = jnp.sum(lax.all_gather(partial_sum, 'mem'), axis=0)]
    psum x1 -> x0, waiting for transfers between devices: 39.6 us -> none  [per_device(): increment = lax.psum(partial_sum, 'mem')]
    reduce_sum x0 -> x1, other arithmetic: none -> 2.67 us  [per_device(): increment = jnp.sum(lax.all_gather(partial_sum, 'mem'), axis=0)]
    unnamed x37 -> x34, local copies, waits for them, and re-layouts: 3.27 us -> 2.46 us
  transfers between devices with their start and end apart: 7 -> 7, of which waited for: 5 -> 5; matrix products, arithmetic and copies ran while one was open for 5% -> 4% of each run, Pallas kernels for 0% -> 0%
where the time goes in v1:
time: 134 us; the launch traced here: 133 us
  waiting for transfers between devices  67.8 us (51%)
  other arithmetic  34.9 us (26%)
  between operations  14.5 us (11%)
  local copies, waits for them, and re-layouts  9.67 us (7%)
  starting transfers between devices  6.56 us (5%)
    all_gather x1, waiting for transfers between devices, per_device(): increment = jnp.sum(lax.all_gather(partial_sum, 'mem'), axis=0)  50.4 us
    sub x7, other arithmetic, diffuse(): interior + zonal_flux[:, :, 1:] - zonal_flux[:, :, :-1] + north_flux  11.5 us
    ppermute x3, waiting for transfers between devices, extended(): lax.ppermute(tail, axis, [(i, (i + 1) % count) for i in range(count)])  9.6 us
    mul x8, other arithmetic, diffuse(): merid_face[:, :, :-1] * (interior[:, :, :, 1:] - interior[:, :, :, :-1])  9.07 us
    ppermute x3, waiting for transfers between devices, extended(): lax.ppermute(head, axis, [((i + 1) % count, i) for i in range(count)])  7.87 us
    ppermute x3, starting transfers between devices, extended(): lax.ppermute(tail, axis, [(i, (i + 1) % count) for i in range(count)])  6.4 us
    mul x9, other arithmetic, diffuse(): zonal_flux = zonal_face * (field[:, :, 1:] - field[:, :, :-1])  4.23 us
    add x1, other arithmetic, per_device(): gradient = alpha + adjoint_field  2.88 us
  transfers between devices with their start and end apart: 7, of which 5 were waited for; matrix products, arithmetic and copies ran while one was open for 4% of the time, Pallas kernels for 0%

profile of v1, /device:TPU:1, one launch (start us, length us, event | category | flops | bytes accessed | tf_op | source)
XLA Modules:
  0.0 133.5 jit_solution(4673400745367270359)
XLA Ops:
  7.2 1.1 fusion.38
  8.3 2.6 %collective-permute-start.2 = (f32[2,8,4,384]{3,2,1,0:T(4,128)S(1)}, f32[2,8,4,384]{3,2,1,0:T(4,128)S(1)}, u32[]{:S(2)}, u32[]{:S(2)}) collective-permute-start(f32[2,8,4,384]{3,2,1,0:T(4,128)S(1)} %get-tuple-element.8), channel_id=1, source_target_pairs={{0,1},{1,2},{2,3},{3,4},{4,5},{5,6},{6,7},{7,0},{8,9},{9,10},{10,1... | collective-permute-start | bytes 294920 | tf_op jit(solution)/shard_map/ppermute | solution.py:16
  11.0 1.5 %fusion.37 = (f32[8,8,4,384]{3,2,1,0:T(4,128)S(1)}, f32[8,8,4,384]{3,2,1,0:T(4,128)S(1)}) fusion(f32[8,8,24,384]{3,2,1,0:T(8,128)} %param.5), kind=kLoop, calls=%fused_computation.83 | loop fusion | bytes 1572864 | tf_op jit(solution)/shard_map/slice | solution.py:13
  12.5 1.8 %collective-permute-start = (f32[8,8,4,384]{3,1,2,0:T(8,128)S(1)}, f32[8,8,4,384]{3,1,2,0:T(8,128)S(1)}, u32[]{:S(2)}, u32[]{:S(2)}) collective-permute-start(f32[8,8,4,384]{3,1,2,0:T(8,128)S(1)} %copy.29), channel_id=1, source_target_pairs={{0,1},{1,2},{2,3},{3,4},{4,5},{5,6},{6,7},{7,0},{8,9},{9,10},{10,1... | collective-permute-start | bytes 1179656 | tf_op jit(solution)/shard_map/ppermute | solution.py:16
  15.5 0.8 slice_bitcast_fusion.2
  16.2 0.8 slice_bitcast_fusion.3
  17.8 0.8 slice_bitcast_fusion.1
  18.7 2.6 %collective-permute-done = f32[8,8,4,384]{3,1,2,0:T(8,128)S(1)} collective-permute-done((f32[8,8,4,384]{3,1,2,0:T(8,128)S(1)}, f32[8,8,4,384]{3,1,2,0:T(8,128)S(1)}, u32[]{:S(2)}, u32[]{:S(2)}) %collective-permute-start) | collective-permute-done | bytes 393248 | tf_op jit(solution)/shard_map/ppermute | solution.py:16
  21.4 4.5 %collective-permute-done.1 = f32[8,8,4,384]{3,1,2,0:T(8,128)S(1)} collective-permute-done((f32[8,8,4,384]{3,1,2,0:T(8,128)S(1)}, f32[8,8,4,384]{3,1,2,0:T(8,128)S(1)}, u32[]{:S(2)}, u32[]{:S(2)}) %collective-permute-start.1) | collective-permute-done | bytes 393248 | tf_op jit(solution)/shard_map/ppermute | solution.py:18
  26.5 1.2 fusion.24
  28.2 1.7 %fusion.26 = f32[8,8,30,384]{3,2,1,0:T(8,128)S(1)} fusion(f32[8,8,31,384]{3,2,1,0:T(8,128)S(1)} %fusion.27, f32[8,8,32,384]{3,2,1,0:T(8,128)S(1)} %pad_maximum_fusion, f32[8,8,30,383]{3,2,1,0:T(8,128)S(1)} %fusion.24), kind=kLoop, calls=%fused_computation.52 | loop fusion | flops 2949120 | bytes 14737920 | tf_op jit(solution)/shard_map/sub | solution.py:36
  29.9 1.2 fusion.20
  31.7 1.7 %fusion.22 = f32[8,8,28,384]{3,2,1,0:T(8,128)S(1)} fusion(f32[8,8,29,384]{3,2,1,0:T(8,128)S(1)} %fusion.23, f32[8,8,30,384]{3,2,1,0:T(8,128)S(1)} %fusion.26, f32[8,8,28,383]{3,2,1,0:T(8,128)S(1)} %fusion.20), kind=kLoop, calls=%fused_computation.44 | loop fusion | flops 2752512 | bytes 13755392 | tf_op jit(solution)/shard_map/sub | solution.py:36
  33.4 1.2 fusion.16
  35.2 1.7 %fusion.18 = f32[8,8,26,384]{3,2,1,0:T(8,128)S(1)} fusion(f32[8,8,27,384]{3,2,1,0:T(8,128)S(1)} %fusion.19, f32[8,8,28,384]{3,2,1,0:T(8,128)S(1)} %fusion.22, f32[8,8,26,383]{3,2,1,0:T(8,128)S(1)} %fusion.16), kind=kLoop, calls=%fused_computation.36 | loop fusion | flops 2555904 | bytes 12772864 | tf_op jit(solution)/shard_map/sub | solution.py:36
  37.8 1.1 fusion.32
  38.9 1.2 fusion.34
  40.6 1.3 fusion
  41.9 50.4 %all-gather.3.cloned.1.call-done = f32[8,8,24,384]{3,2,1,0:T(8,128)} async-done(((f32[2,8,24,384]{3,2,1,0:T(8,128)}), f32[8,8,24,384]{3,2,1,0:T(8,128)}) %all-gather.3.cloned.1.call-update) | async-done | bytes 2359312 | tf_op jit(solution)/shard_map/all_gather | solution.py:45
  92.3 2.7 %reduce_sum.28 = f32[2,8,24,384]{3,2,1,0:T(8,128)} reduce(f32[4,2,8,24,384]{4,3,2,1,0:T(8,128)} %bitcast.29, f32[]{:T(128)} %constant.1.clone.1), dimensions={0}, to_apply=%region_1.0 | reduce | flops 442368 | bytes 2949124 | tf_op jit(solution)/shard_map/reduce_sum | solution.py:45
  95.0 1.6 %subtract_multiply_fusion = f32[2,8,24,384]{3,2,1,0:T(8,128)S(1)} fusion(f32[2,8,24,384]{3,2,1,0:T(8,128)} %param.8, f32[2,8,24,384]{3,2,1,0:T(8,128)} %reduce_sum.28, f32[2,8,24,384]{3,2,1,0:T(8,128)} %param.7), kind=kLoop, calls=%fused_computation.72 | loop fusion | flops 294912 | bytes 2359296 | tf_op jit(solution)/shard_map/mul | solution.py:46
  97.9 2.0 %collective-permute-start.4 = (f32[8,8,4,384]{3,1,2,0:T(8,128)S(1)}, f32[8,8,4,384]{3,1,2,0:T(8,128)S(1)}, u32[]{:S(2)}, u32[]{:S(2)}) collective-permute-start(f32[8,8,4,384]{3,1,2,0:T(8,128)S(1)} %copy.25), channel_id=1, source_target_pairs={{0,1},{1,2},{2,3},{3,4},{4,5},{5,6},{6,7},{7,0},{8,9},{9,10},{10,1... | collective-permute-start | bytes 1179656 | tf_op jit(solution)/shard_map/ppermute | solution.py:16
  100.0 7.0 %collective-permute-done.4 = f32[8,8,4,384]{3,1,2,0:T(8,128)S(1)} collective-permute-done((f32[8,8,4,384]{3,1,2,0:T(8,128)S(1)}, f32[8,8,4,384]{3,1,2,0:T(8,128)S(1)}, u32[]{:S(2)}, u32[]{:S(2)}) %collective-permute-start.4) | collective-permute-done | bytes 393248 | tf_op jit(solution)/shard_map/ppermute | solution.py:16
  107.1 3.4 %collective-permute-done.5 = f32[8,8,4,384]{3,1,2,0:T(8,128)S(1)} collective-permute-done((f32[8,8,4,384]{3,1,2,0:T(8,128)S(1)}, f32[8,8,4,384]{3,1,2,0:T(8,128)S(1)}, u32[]{:S(2)}, u32[]{:S(2)}) %collective-permute-start.5) | collective-permute-done | bytes 393248 | tf_op jit(solution)/shard_map/ppermute | solution.py:18
  111.5 1.2 fusion.11
  113.2 1.7 %fusion.13 = f32[8,8,30,384]{3,2,1,0:T(8,128)S(1)} fusion(f32[8,8,31,384]{3,2,1,0:T(8,128)S(1)} %fusion.14, f32[8,8,32,384]{3,2,1,0:T(8,128)S(1)} %pad_maximum_fusion.1, f32[8,8,30,383]{3,2,1,0:T(8,128)S(1)} %fusion.11), kind=kLoop, calls=%fused_computation.26 | loop fusion | flops 2949120 | bytes 14737920 | tf_op jit(solution)/shard_map/sub | solution.py:36
  115.0 1.2 fusion.7
  116.7 1.7 %fusion.9 = f32[8,8,28,384]{3,2,1,0:T(8,128)S(1)} fusion(f32[8,8,29,384]{3,2,1,0:T(8,128)S(1)} %fusion.10, f32[8,8,30,384]{3,2,1,0:T(8,128)S(1)} %fusion.13, f32[8,8,28,383]{3,2,1,0:T(8,128)S(1)} %fusion.7), kind=kLoop, calls=%fused_computation.18 | loop fusion | flops 2752512 | bytes 13755392 | tf_op jit(solution)/shard_map/sub | solution.py:36
  118.4 1.2 fusion.3
  120.2 1.7 %fusion.5 = f32[8,8,26,384]{3,2,1,0:T(8,128)S(1)} fusion(f32[8,8,27,384]{3,2,1,0:T(8,128)S(1)} %fusion.6, f32[8,8,28,384]{3,2,1,0:T(8,128)S(1)} %fusion.9, f32[8,8,26,383]{3,2,1,0:T(8,128)S(1)} %fusion.3), kind=kLoop, calls=%fused_computation.10 | loop fusion | flops 2555904 | bytes 12772864 | tf_op jit(solution)/shard_map/sub | solution.py:36
  122.8 0.9 fusion.28
  123.8 2.9 %fusion.31 = f32[8,8,24,384]{3,2,1,0:T(8,128)} fusion(f32[8,8,24,384]{3,2,1,0:T(8,128)S(1)} %copy-done, f32[8,8,25,384]{3,2,1,0:T(8,128)S(1)} %fusion.2, f32[8,8,26,384]{3,2,1,0:T(8,128)S(1)} %fusion.5, f32[8,8,24,383]{3,2,1,0:T(8,128)S(1)} %fusion.28), kind=kLoop, calls=%fused_computation.63 | loop fusion | flops 2949120 | bytes 14149632 | tf_op jit(solution)/shard_map/add | solution.py:50
  (65 shorter events, 10.8 us)
Async XLA Ops:
  7.2 7.3 %copy-start.3 = (f32[2,8,24,384]{3,2,1,0:T(8,128)S(1)}, f32[2,8,24,384]{3,2,1,0:T(8,128)}, u32[]{:S(2)}) copy-start(f32[2,8,24,384]{3,2,1,0:T(8,128)} %param.9) | copy-start | bytes 1769476
  7.2 85.1 %all-gather.3.cloned.1.call-start = ((), (), s32[]{:S(2)}) async-start(), calls=%async_computation | async-start | bytes 2949120 | tf_op jit(solution)/shard_map/all_gather | solution.py:45
  8.3 6.9 %collective-permute-start.2 = (f32[2,8,4,384]{3,2,1,0:T(4,128)S(1)}, f32[2,8,4,384]{3,2,1,0:T(4,128)S(1)}, u32[]{:S(2)}, u32[]{:S(2)}) collective-permute-start(f32[2,8,4,384]{3,2,1,0:T(4,128)S(1)} %get-tuple-element.8), channel_id=1, source_target_pairs={{0,1},{1,2},{2,3},{3,4},{4,5},{5,6},{6,7},{7,0},{8,9},{9,10},{10,1... | collective-permute-start | bytes 294920 | tf_op jit(solution)/shard_map/ppermute | solution.py:16
  11.0 4.3 %collective-permute-start.3 = (f32[2,8,4,384]{3,2,1,0:T(4,128)S(1)}, f32[2,8,4,384]{3,2,1,0:T(4,128)S(1)}, u32[]{:S(2)}, u32[]{:S(2)}) collective-permute-start(f32[2,8,4,384]{3,2,1,0:T(4,128)S(1)} %get-tuple-element.9), channel_id=1, source_target_pairs={{1,0},{2,1},{3,2},{4,3},{5,4},{6,5},{7,6},{0,7},{9,8},{10,9},{11,1... | collective-permute-start | bytes 294920 | tf_op jit(solution)/shard_map/ppermute | solution.py:18
  12.5 8.7 %collective-permute-start = (f32[8,8,4,384]{3,1,2,0:T(8,128)S(1)}, f32[8,8,4,384]{3,1,2,0:T(8,128)S(1)}, u32[]{:S(2)}, u32[]{:S(2)}) collective-permute-start(f32[8,8,4,384]{3,1,2,0:T(8,128)S(1)} %copy.29), channel_id=1, source_target_pairs={{0,1},{1,2},{2,3},{3,4},{4,5},{5,6},{6,7},{7,0},{8,9},{9,10},{10,1... | collective-permute-start | bytes 1179656 | tf_op jit(solution)/shard_map/ppermute | solution.py:16
  14.4 11.5 %collective-permute-start.1 = (f32[8,8,4,384]{3,1,2,0:T(8,128)S(1)}, f32[8,8,4,384]{3,1,2,0:T(8,128)S(1)}, u32[]{:S(2)}, u32[]{:S(2)}) collective-permute-start(f32[8,8,4,384]{3,1,2,0:T(8,128)S(1)} %copy.30), channel_id=1, source_target_pairs={{1,0},{2,1},{3,2},{4,3},{5,4},{6,5},{7,6},{0,7},{9,8},{10,9},{11,1... | collective-permute-start | bytes 1179656 | tf_op jit(solution)/shard_map/ppermute | solution.py:18
  15.4 11.1 %copy-start.12 = (f32[8,30,384]{2,1,0:T(8,128)}, f32[8,30,384]{2,1,0:T(8,128)S(1)}, u32[]{:S(2)}) copy-start(f32[8,30,384]{2,1,0:T(8,128)S(1)} %slice_bitcast_fusion.4) | copy-start | bytes 1105924
  15.4 10.5 %copy-start = (f32[8,8,24,384]{3,2,1,0:T(8,128)S(1)}, f32[8,8,24,384]{3,2,1,0:T(8,128)}, u32[]{:S(2)}) copy-start(f32[8,8,24,384]{3,2,1,0:T(8,128)} %param.5) | copy-start | bytes 7077892
  15.5 12.2 %copy-start.10 = (f32[8,31,384]{2,1,0:T(8,128)}, f32[8,31,384]{2,1,0:T(8,128)S(1)}, u32[]{:S(2)}) copy-start(f32[8,31,384]{2,1,0:T(8,128)S(1)} %slice_bitcast_fusion.5) | copy-start | bytes 1142788
  28.2 1.7 %copy-start.9 = (f32[8,28,384]{2,1,0:T(8,128)S(1)}, f32[8,28,384]{2,1,0:T(8,128)}, u32[]{:S(2)}) copy-start(f32[8,28,384]{2,1,0:T(8,128)} %slice_bitcast_fusion.2) | copy-start | bytes 1032196
  29.9 1.2 copy-start.7
  31.7 1.7 %copy-start.4 = (f32[8,26,384]{2,1,0:T(8,128)S(1)}, f32[8,26,384]{2,1,0:T(8,128)}, u32[]{:S(2)}) copy-start(f32[8,26,384]{2,1,0:T(8,128)} %slice_bitcast_fusion) | copy-start | bytes 958468
  33.4 1.2 copy-start.5
  36.9 1.0 copy-start.14
  38.9 1.7 %copy-start.1 = (bf16[2,8,8,24,384]{4,3,2,1,0:T(8,128)(2,1)S(1)}, bf16[2,8,8,24,384]{4,3,2,1,0:T(8,128)(2,1)}, u32[]{:S(2)}) copy-start(bf16[2,8,8,24,384]{4,3,2,1,0:T(8,128)(2,1)} %param.6) | copy-start | bytes 7077892
  95.0 2.2 %copy-start.2 = (bf16[2,8,8,24,384]{4,3,2,1,0:T(8,128)(2,1)S(1)}, bf16[2,8,8,24,384]{4,3,2,1,0:T(8,128)(2,1)}, u32[]{:S(2)}) copy-start(bf16[2,8,8,24,384]{4,3,2,1,0:T(8,128)(2,1)} %param.6) | copy-start | bytes 7077892
  97.9 9.1 %collective-permute-start.4 = (f32[8,8,4,384]{3,1,2,0:T(8,128)S(1)}, f32[8,8,4,384]{3,1,2,0:T(8,128)S(1)}, u32[]{:S(2)}, u32[]{:S(2)}) collective-permute-start(f32[8,8,4,384]{3,1,2,0:T(8,128)S(1)} %copy.25), channel_id=1, source_target_pairs={{0,1},{1,2},{2,3},{3,4},{4,5},{5,6},{6,7},{7,0},{8,9},{9,10},{10,1... | collective-permute-start | bytes 1179656 | tf_op jit(solution)/shard_map/ppermute | solution.py:16
  99.9 10.5 %collective-permute-start.5 = (f32[8,8,4,384]{3,1,2,0:T(8,128)S(1)}, f32[8,8,4,384]{3,1,2,0:T(8,128)S(1)}, u32[]{:S(2)}, u32[]{:S(2)}) collective-permute-start(f32[8,8,4,384]{3,1,2,0:T(8,128)S(1)} %copy.26), channel_id=1, source_target_pairs={{1,0},{2,1},{3,2},{4,3},{5,4},{6,5},{7,6},{0,7},{9,8},{10,9},{11,1... | collective-permute-start | bytes 1179656 | tf_op jit(solution)/shard_map/ppermute | solution.py:18
  110.5 1.0 copy-start.13
  111.5 1.2 copy-start.11
  115.0 1.2 copy-start.8
  118.4 1.2 copy-start.6
  121.9 1.0 copy-start.15
Sparse Core Ops, SparseCore 0:
  42.1 50.1 all-gather.2
